TPU v7x, 32 devices: a whole 2x2x4 slice. The times are simulated.
32 devices in a mesh: group: 2 (over x), src: 8 (over z, y), tile: 2 (over core).
Axes of the slice: x: 2, y: 2, z: 4, core: 2. Of those that a mesh axis runs over, the one named last changes fastest.
Arguments:
- near_field: bfloat16 [4, 64, 2, 3, 512], P(('group', 'tile'), 'src'), parts along dimension 0, may hold values from -6 to 6
- x_taps: bfloat16 [8, 2, 8, 65], P('src'), may hold values from -0.5 to 0.5
- y_taps: bfloat16 [8, 2, 8, 65], P('src'), may hold values from -0.1875 to 0.1875
- source_weight: float32 [8], P('src'), may hold values from 0.0125 to 0.125
Outputs:
- intensity: float32 [4, 64, 512], P(('group', 'tile'), 'src'), parts along dimension 0
There are 2 independent parts, one for each index of `group`. A program takes and returns all parts, laid end to end along the dimension named above; an argument that names none is the same for every part. Nothing has to cross between parts.
All inputs are finite; a program needn't handle non-finite values.
Results may differ from a plain program's by a relative error of at most 0.00054.
Values may be sent and summed in bfloat16 or wider, within the bound.
A program may use at most 128 MiB of HBM per device.

v0:
```python
import jax
import jax.numpy as jnp
from jax import lax
from jax.sharding import PartitionSpec as P


def padded_2(cells, sides, width):
    for axis, dim in sides:
        count = lax.axis_size(axis)
        ends = count - 1
        head = lax.slice_in_dim(cells, 0, width, axis=dim)
        tail = lax.slice_in_dim(cells, cells.shape[dim] - width, cells.shape[dim], axis=dim)
        cells = jnp.concatenate(
            [
                lax.ppermute(tail, axis, [(i, (i + 1) % count) for i in range(ends)]),
                cells,
                lax.ppermute(head, axis, [((i + 1) % count, i) for i in range(ends)]),
            ],
            axis=dim,
        )
    return cells


def column_mats(taps):
    tap_count = taps.shape[-1]
    shift = lax.broadcasted_iota(jnp.int32, (tap_count, 256, 128), 0)
    inner = lax.broadcasted_iota(jnp.int32, (tap_count, 256, 128), 1)
    outer = lax.broadcasted_iota(jnp.int32, (tap_count, 256, 128), 2)
    select = (inner - outer == shift).astype(jnp.float32)
    coef = jnp.einsum(
        "xprt,tqj->xpqrj", taps.astype(jnp.float32), select, precision=lax.Precision.HIGHEST
    )
    real_part, imag_part = (coef[:, 0], coef[:, 1])
    full = jnp.stack(
        [jnp.stack([real_part, imag_part], axis=2), jnp.stack([-imag_part, real_part], axis=2)],
        axis=1,
    ).astype(jnp.bfloat16)
    return (full[:, :, :128], full[:, :, 128:])


def column_pass(rows_field, lower_mat, upper_mat, rim_width):
    count_rows, _, comps, width = rows_field.shape
    padded = jnp.pad(rows_field, ((0, 0), (0, 0), (0, 0), (rim_width, 128 - rim_width)))
    pieces = padded.reshape(count_rows, 2, comps, width // 128 + 1, 128)
    result = jnp.einsum(
        "ipcbq,xpqsrj->ixsrcbj", pieces[:, :, :, :-1], lower_mat, preferred_element_type=jnp.float32
    )
    result = result + jnp.einsum(
        "ipcbq,xpqsrj->ixsrcbj", pieces[:, :, :, 1:], upper_mat, preferred_element_type=jnp.float32
    )
    sources, ranks = (lower_mat.shape[0], lower_mat.shape[4])
    return result.reshape(count_rows, sources, 2, ranks, comps, width).astype(jnp.bfloat16)


def row_matrices(taps, block_rows, rim_width):
    tap_count = taps.shape[-1]
    span = block_rows + 2 * rim_width
    shift = lax.broadcasted_iota(jnp.int32, (tap_count, block_rows, span), 0)
    out_row = lax.broadcasted_iota(jnp.int32, (tap_count, block_rows, span), 1)
    in_row = lax.broadcasted_iota(jnp.int32, (tap_count, block_rows, span), 2)
    select = (in_row - out_row == shift).astype(jnp.float32)
    coef = jnp.einsum(
        "xprt,tik->xpirk", taps.astype(jnp.float32), select, precision=lax.Precision.HIGHEST
    )
    real_part, imag_part = (coef[:, 0], coef[:, 1])
    full = jnp.stack(
        [jnp.stack([real_part, -imag_part], axis=2), jnp.stack([imag_part, real_part], axis=2)],
        axis=1,
    )
    return full.astype(jnp.bfloat16)


def per_device(near_field, x_taps, y_taps, source_weight):
    rim_width = (x_taps.shape[-1] - 1) // 2
    width = near_field.shape[-1]
    local_rows = near_field.shape[1]
    whole_tile = lax.all_gather(near_field, "src", axis=1, tiled=True)
    padded_field = padded_2(whole_tile, (("tile", 1),), rim_width)
    lower_mat, upper_mat = column_mats(x_taps)
    padded_pass = column_pass(padded_field[0], lower_mat, upper_mat, rim_width)
    tile_rows = padded_pass.shape[0] - 2 * rim_width
    block_rows = 64
    row_mats = row_matrices(y_taps, block_rows, rim_width)

    def one_block(index):
        first_row = index * block_rows
        window = lax.dynamic_slice_in_dim(padded_pass, first_row, block_rows + 2 * rim_width, 0)
        image = jnp.einsum(
            "xoiprk,kxprcw->xoicw", row_mats, window, preferred_element_type=jnp.float32
        )
        power = jnp.sum(image * image, axis=(1, 3))
        return jnp.sum(source_weight[:, None, None] * power, axis=0)

    blocks = lax.map(one_block, jnp.arange(tile_rows // block_rows, dtype=jnp.int32))
    own_image = blocks.reshape(tile_rows, width)
    summed = lax.psum_scatter(own_image, "src", scatter_dimension=0, tiled=True)
    return summed.reshape(1, local_rows, width)


def solution(mesh):
    placed = (
        P(("group", "tile"), "src", None, None, None),
        P("src", None, None, None),
        P("src", None, None, None),
        P("src"),
    )
    return jax.shard_map(
        per_device,
        mesh=mesh,
        in_specs=placed,
        out_specs=P(("group", "tile"), "src", None),
        check_vma=False,
    )
```

profile of v0, /device:TPU:0, one launch (start us, length us, event | category | flops | bytes accessed | tf_op | source)
XLA Modules:
  0.0 142.8 jit_solution(395169081686979123)
XLA Ops:
  6.5 0.0 copy-start
  6.5 0.0 reduce-scatter.2.cloned.1.call-start
  6.5 33.1 %all_gather.3 = bf16[1,64,2,3,512]{4,2,3,0,1:T(2,128)(2,1)S(1)} all-gather(bf16[1,8,2,3,512]{4,2,3,0,1:T(2,128)(2,1)} %bitcast.120), channel_id=1, replica_groups=mesh['group'=2,'src'=8,'tile'=2] {'src'}, dimensions={1}, use_global_device_ids=true | all-gather | bytes 442368 | tf_op jit(solution)/shard_map/all_gather | solution.py:77
  39.6 0.3 fusion.45
  39.9 0.7 copy.29
  40.6 2.0 %collective-permute-start = (bf16[1,32,2,3,512]{4,1,3,2,0:T(8,128)(2,1)}, bf16[1,32,2,3,512]{4,1,3,2,0:T(8,128)(2,1)}, u32[]{:S(2)}, u32[]{:S(2)}) collective-permute-start(bf16[1,32,2,3,512]{4,1,3,2,0:T(8,128)(2,1)} %copy.29), channel_id=1, source_target_pairs={{0,1},{2,3},{4,5},{6,7},{8,9},{10,11},{12,13},{14,15},{16,17},{18,... | collective-permute-start | bytes 589832 | tf_op jit(solution)/shard_map/ppermute | solution.py:15
  42.6 0.7 copy.30
  43.3 1.3 collective-permute-start.1
  44.6 0.0 copy-done
  44.6 1.1 fusion.9
  45.7 0.0 copy-start.2
  45.7 0.1 fusion.36
  45.9 0.1 fusion.35
  45.9 0.5 copy-done.2
  46.4 0.5 fusion.18
  47.0 1.1 maximum_bitcast_fusion.1
  48.1 0.8 maximum_bitcast_fusion.3
  49.0 1.3 copy.32
  50.9 1.4 fusion.26
  52.3 0.0 copy-start.1
  52.3 0.0 collective-permute-done
  52.3 2.2 %copy.31 = bf16[1,32,2,3,512]{1,4,3,2,0:T(8,128)(2,1)} copy(bf16[1,32,2,3,512]{4,1,3,2,0:T(8,128)(2,1)} %collective-permute-done) | data formatting | bytes 393216 | tf_op jit(solution)/shard_map/ppermute | solution.py:15
  54.5 0.0 collective-permute-done.1
  54.5 2.1 %copy.33 = bf16[1,32,2,3,512]{1,4,3,2,0:T(8,128)(2,1)} copy(bf16[1,32,2,3,512]{4,1,3,2,0:T(8,128)(2,1)} %collective-permute-done.1) | data formatting | bytes 393216 | tf_op jit(solution)/shard_map/ppermute | solution.py:17
  56.6 0.0 copy-done.1
  56.6 2.1 %maximum_bitcast_fusion.2 = bf16[128,2,3,512]{0,3,2,1:T(8,128)(2,1)S(1)} fusion(bf16[1,32,2,3,512]{1,4,3,2,0:T(8,128)(2,1)} %copy.33, bf16[1,64,2,3,512]{1,4,3,2,0:T(8,128)(2,1)S(1)} %copy-done.1, bf16[1,32,2,3,512]{1,4,3,2,0:T(8,128)(2,1)} %copy.31), kind=kLoop, calls=%fused_computation.31 | loop fusion | flops 2359296 | bytes 1572864 | tf_op jit(solution)/shard_map/squeeze | solution.py:80
  58.7 0.1 pad.4
  58.8 1.1 fusion.44
  59.9 1.2 copy.61
  61.1 1.5 %copy.62 = bf16[128,2,3,4,128]{4,0,1,3,2:T(8,128)(2,1)S(1)} copy(bf16[128,2,3,4,128]{0,4,3,2,1:T(8,128)(2,1)} %get-tuple-element.24) | data formatting | bytes 1572864
  62.6 3.0 %fusion.29 = f32[2,8,128,128,3,4,1]{3,2,6,5,4,1,0:T(8,128)S(1)} fusion(bf16[2,128,2,8,128,1,1]{4,3,1,2,0,6,5:T(8,128)(2,1)S(1)} %get-tuple-element.14, bf16[128,2,3,4,128]{4,0,1,3,2:T(8,128)(2,1)} %copy.61), kind=kOutput, calls=%fused_computation.26 | convolution fusion | flops 1610612736 | bytes 14417920 | tf_op jit(solution)/shard_map/ipcbq,xpqsrj->ixsrcbj/dot_general | solution.py:45
  65.6 2.3 %fusion = bf16[2,8,128,128,3,4]{3,2,5,4,1,0:T(8,128)(2,1)S(1)} fusion(f32[2,8,128,128,3,4,1]{3,2,6,5,4,1,0:T(8,128)S(1)} %fusion.29, bf16[2,128,2,8,128,1,1]{4,3,1,2,0,6,5:T(8,128)(2,1)S(1)} %get-tuple-element.13, bf16[128,2,3,4,128]{4,0,1,3,2:T(8,128)(2,1)S(1)} %copy.62), kind=kOutput, calls=%fused_computation.1 | convolution fusion | flops 1616904192 | bytes 20709376 | tf_op jit(solution)/shard_map/ipcbq,xpqsrj->ixsrcbj/dot_general | solution.py:48
  67.9 3.2 %fusion.21 = f32[64,512]{1,0:T(8,128)S(1)} fusion(bf16[128,2,8,3,512,1]{0,4,3,2,1,5:T(8,128)(2,1)S(1)} %bitcast.119, bf16[2,64,2,8,128,1]{4,3,1,2,0,5:T(8,128)(2,1)} %maximum_bitcast_fusion.3), kind=kOutput, calls=%fused_computation.16 | convolution fusion | flops 805666816 | bytes 6946816 | tf_op jit(solution)/shard_map/while/body/eval_jaxpr/xoiprk,kxprcw->xoicw/dot_general | solution.py:88
  71.1 0.7 broadcast_multiply_fusion
  71.8 0.0 reduce-scatter.2.cloned.1.call-update
  71.8 64.1 %reduce-scatter.2.cloned.1.call-done = f32[8,512]{1,0:T(8,128)} async-done(((f32[64,512]{1,0:T(8,128)}), f32[8,512]{1,0:T(8,128)}) %reduce-scatter.2.cloned.1.call-update) | async-done | bytes 16400 | tf_op jit(solution)/shard_map/reduce_scatter | solution.py:96
  (2 shorter events, 0.1 us)
Async XLA Ops:
  6.5 38.0 %copy-start = (bf16[1,2,8,65]{3,2,1,0:T(8,128)(2,1)S(1)}, bf16[1,2,8,65]{3,2,1,0:T(8,128)(2,1)}, u32[]{:S(2)}) copy-start(bf16[1,2,8,65]{3,2,1,0:T(8,128)(2,1)} %param.5) | copy-start | bytes 6244
  6.5 129.4 %reduce-scatter.2.cloned.1.call-start = ((), (), s32[]{:S(2)}) async-start(), calls=%async_computation.1 | async-start | bytes 147456 | tf_op jit(solution)/shard_map/reduce_scatter | solution.py:96
  40.6 11.8 %collective-permute-start = (bf16[1,32,2,3,512]{4,1,3,2,0:T(8,128)(2,1)}, bf16[1,32,2,3,512]{4,1,3,2,0:T(8,128)(2,1)}, u32[]{:S(2)}, u32[]{:S(2)}) collective-permute-start(bf16[1,32,2,3,512]{4,1,3,2,0:T(8,128)(2,1)} %copy.29), channel_id=1, source_target_pairs={{0,1},{2,3},{4,5},{6,7},{8,9},{10,11},{12,13},{14,15},{16,17},{18,... | collective-permute-start | bytes 589832 | tf_op jit(solution)/shard_map/ppermute | solution.py:15
  43.3 11.2 %collective-permute-start.1 = (bf16[1,32,2,3,512]{4,1,3,2,0:T(8,128)(2,1)}, bf16[1,32,2,3,512]{4,1,3,2,0:T(8,128)(2,1)}, u32[]{:S(2)}, u32[]{:S(2)}) collective-permute-start(bf16[1,32,2,3,512]{4,1,3,2,0:T(8,128)(2,1)} %copy.30), channel_id=1, source_target_pairs={{1,0},{3,2},{5,4},{7,6},{9,8},{11,10},{13,12},{15,14},{17,16},{19,... | collective-permute-start | bytes 589832 | tf_op jit(solution)/shard_map/ppermute | solution.py:17
  45.7 0.7 copy-start.2
  52.3 4.3 %copy-start.1 = (bf16[1,64,2,3,512]{1,4,3,2,0:T(8,128)(2,1)S(1)}, bf16[1,64,2,3,512]{1,4,3,2,0:T(8,128)(2,1)}, u32[]{:S(2)}) copy-start(bf16[1,64,2,3,512]{1,4,3,2,0:T(8,128)(2,1)} %copy.32) | copy-start | bytes 1179652
Sparse Core Ops, SparseCore 0:
  71.9 63.9 reduce-scatter.1
where the time goes:
time: 143 us
  waiting for transfers between devices  64.1 us (45%)
  blocking collectives  33.1 us (23%)
  between operations  14.2 us (10%)
  local copies, waits for them, and re-layouts  11.8 us (8%)
  matrix products  10.1 us (7%)
  other arithmetic  6.23 us (4%)
  starting transfers between devices  3.26 us (2%)
    reduce_scatter x1, waiting for transfers between devices, per_device(): summed = lax.psum_scatter(own_image, 'src', scatter_dimension=0, tiled=True)  64.1 us
    all_gather x1, blocking collectives, per_device(): whole_tile = lax.all_gather(near_field, 'src', axis=1, tiled=True)  33.1 us
    dot_general x1, matrix products, one_block(): jnp.einsum('xoiprk,kxprcw->xoicw', row_mats, window, preferred_element_ty...  3.22 us
    unnamed x8, local copies, waits for them, and re-layouts  3.17 us
    dot_general x1, matrix products, column_pass(): jnp.einsum('ipcbq,xpqsrj->ixsrcbj', pieces[:, :, :, :-1], lower_mat, pref...  2.99 us
  transfers between devices with their start and end apart: 3, of which 1 were waited for; matrix products, arithmetic and copies ran while one was open for 7% of the time, Pallas kernels for 0%

commit v1 on v0

v1 whole, which is shorter than its diff:
```python
import functools

import jax
import jax.numpy as jnp
from jax import lax
from jax.experimental import pallas as pl
from jax.experimental.pallas import tpu as pltpu
from jax.sharding import PartitionSpec as P

MESH = pl.DeviceIdType.MESH
BLOCK = 64
WINDOW = 128
NT = (((1,), (1,)), ((), ()))


def toeplitz(row):
    spread = jnp.broadcast_to(row, (BLOCK, WINDOW))
    return pltpu.roll(spread, 0, 1, stride=1, stride_axis=0)


def kernel(dims, field_ref, taps_ref, out_ref, window, taps_all, field32, fields,
           col_mat, row_mat, passed, acc, mine, gathered,
           f_send, f_recv, f_self, t_send, t_recv, t_self, o_send, o_recv):
    n_src, n_tile, local_rows, comps, ranks, tap_count = dims
    slots = WINDOW // local_rows
    per_group = BLOCK // local_rows
    halo = (WINDOW - BLOCK) // 2 // local_rows
    col_blocks = field_ref.shape[0]
    groups = n_src // per_group
    me = lax.axis_index("src")
    tile = lax.axis_index("tile")
    flat = tile * n_src + me
    devices = n_src * n_tile

    barrier = pltpu.get_barrier_semaphore()

    def greet(step, carry):
        other = lax.rem(flat + step, devices)
        pl.semaphore_signal(
            barrier, inc=1, device_id={"src": lax.rem(other, n_src), "tile": other // n_src},
            device_id_type=MESH)
        return carry

    lax.fori_loop(1, devices, greet, 0)
    pl.semaphore_wait(barrier, devices - 1)

    own_group = flat // per_group
    place = lax.rem(flat, per_group)
    upper = place >= per_group - halo
    second = jnp.where(upper, own_group + 1, own_group - 1)
    second_ok = jnp.logical_and(second >= 0, second < groups * n_tile)
    my_col = lax.rem(me, col_blocks)
    my_row = me // col_blocks

    def field_copy(col, row_group, slot, sem):
        to_tile = row_group // groups
        to_src = lax.rem(row_group, groups) * col_blocks + col
        return pltpu.make_async_remote_copy(
            src_ref=field_ref.at[col], dst_ref=window.at[slot],
            send_sem=f_send.at[sem], recv_sem=f_recv.at[slot],
            device_id={"src": to_src, "tile": to_tile}, device_id_type=MESH)

    first_slot = place + halo
    second_slot = jnp.where(upper, place + halo - per_group, place + halo + per_group)
    self_copy = pltpu.make_async_copy(field_ref.at[my_col], window.at[first_slot], f_self)
    self_taps = pltpu.make_async_copy(taps_ref, taps_all.at[me], t_self)

    def is_self(col):
        return own_group * col_blocks + col == flat

    def taps_copy(step):
        return pltpu.make_async_remote_copy(
            src_ref=taps_ref, dst_ref=taps_all.at[me],
            send_sem=t_send.at[step], recv_sem=t_recv.at[me],
            device_id={"src": lax.rem(me + step, n_src)}, device_id_type=MESH)

    self_copy.start()
    self_taps.start()

    def send_fields(step, carry):
        col = lax.rem(my_col + step, col_blocks)

        @pl.when(jnp.logical_not(is_self(col)))
        def _():
            field_copy(col, own_group, first_slot, step).start()

        @pl.when(second_ok)
        def _():
            field_copy(col, second, second_slot, col_blocks + step).start()

        return carry

    lax.fori_loop(0, col_blocks, send_fields, 0)

    def send_taps(step, carry):
        taps_copy(step).start()
        return carry

    lax.fori_loop(1, n_src, send_taps, 0)

    first_block = (tile * groups + my_row) * per_group - halo
    self_copy.wait()
    for slot in range(slots):
        block = first_block + slot
        ok = jnp.logical_and(block >= 0, block < devices)

        @pl.when(jnp.logical_and(ok, block != flat))
        def _():
            pltpu.make_async_remote_copy(
                src_ref=window.at[slot], dst_ref=window.at[slot],
                send_sem=f_send.at[0], recv_sem=f_recv.at[slot],
                device_id={"src": me}, device_id_type=MESH).wait_recv()

        rows = pl.ds(slot * local_rows, local_rows)

        @pl.when(ok)
        def _():
            got = window[slot].astype(jnp.float32)
            for part in range(2 * comps):
                field32[part, rows, :] = got[part * local_rows:(part + 1) * local_rows]

        @pl.when(jnp.logical_not(ok))
        def _():
            for part in range(2 * comps):
                field32[part, rows, :] = jnp.zeros((local_rows, WINDOW), jnp.float32)

    for comp in range(comps):
        real = field32[2 * comp]
        imag = field32[2 * comp + 1]
        top = pl.ds(comp * WINDOW, WINDOW)
        low = pl.ds((comps + comp) * WINDOW, WINDOW)
        fields[top, :WINDOW] = real.astype(jnp.bfloat16)
        fields[top, WINDOW:] = (-imag).astype(jnp.bfloat16)
        fields[low, :WINDOW] = imag.astype(jnp.bfloat16)
        fields[low, WINDOW:] = real.astype(jnp.bfloat16)

    self_taps.wait()

    def wait_taps(step, carry):
        source = lax.rem(me + step, n_src)
        pltpu.make_async_remote_copy(
            src_ref=taps_ref, dst_ref=taps_all.at[source],
            send_sem=t_send.at[step], recv_sem=t_recv.at[source],
            device_id={"src": source}, device_id_type=MESH).wait_recv()
        return carry

    lax.fori_loop(1, n_src, wait_taps, 0)

    acc[...] = jnp.zeros_like(acc)
    lane = lax.broadcasted_iota(jnp.int32, (4 * ranks, WINDOW), 1)

    def one_source(source, carry):
        raw = taps_all[source].astype(jnp.float32)
        taps = jnp.where(lane < tap_count, raw, 0.0)
        weight = jnp.sum(
            jnp.where(lane[0:1] >= WINDOW - 3, raw[0:1], 0.0), axis=1, keepdims=True)
        for rank in range(ranks):
            across = pl.ds(rank * BLOCK, BLOCK)
            for part in range(2):
                index = part * ranks + rank
                col_mat[across, part * WINDOW:(part + 1) * WINDOW] = toeplitz(
                    taps[index:index + 1]).astype(jnp.bfloat16)
            real = toeplitz(taps[2 * ranks + rank:2 * ranks + rank + 1])
            imag = toeplitz(taps[3 * ranks + rank:3 * ranks + rank + 1])
            base = 2 * rank * WINDOW
            row_mat[:BLOCK, base:base + WINDOW] = real.astype(jnp.bfloat16)
            row_mat[:BLOCK, base + WINDOW:base + 2 * WINDOW] = (-imag).astype(jnp.bfloat16)
            row_mat[BLOCK:, base:base + WINDOW] = imag.astype(jnp.bfloat16)
            row_mat[BLOCK:, base + WINDOW:base + 2 * WINDOW] = real.astype(jnp.bfloat16)
        for pair in range(comps):
            some = lax.dot_general(
                col_mat[...], fields[2 * pair * WINDOW:2 * (pair + 1) * WINDOW, :], NT,
                preferred_element_type=jnp.float32).astype(jnp.bfloat16)
            for half in range(2):
                part, comp = divmod(2 * pair + half, comps)
                for rank in range(ranks):
                    base = (2 * rank + part) * WINDOW
                    passed[comp * BLOCK:(comp + 1) * BLOCK, base:base + WINDOW] = some[
                        rank * BLOCK:(rank + 1) * BLOCK, half * WINDOW:(half + 1) * WINDOW]
        image = lax.dot_general(
            passed[...], row_mat[...], NT, preferred_element_type=jnp.float32)
        power = image * image
        total = power[:BLOCK]
        for comp in range(1, comps):
            total = total + power[comp * BLOCK:(comp + 1) * BLOCK]
        acc[:BLOCK, :] += weight * total
        return carry

    lax.fori_loop(0, n_src, one_source, 0)

    turned = acc[...].T
    block_image = turned[:BLOCK] + turned[BLOCK:]
    for owner in range(per_group):
        mine[owner] = block_image[owner * local_rows:(owner + 1) * local_rows]

    my_place = lax.rem(me, per_group)

    def out_copy(step):
        owner = lax.rem(my_place + step, per_group)
        return pltpu.make_async_remote_copy(
            src_ref=mine.at[owner], dst_ref=gathered.at[my_col],
            send_sem=o_send.at[step], recv_sem=o_recv.at[my_col],
            device_id={"src": my_row * per_group + owner}, device_id_type=MESH)

    def send_out(step, carry):
        out_copy(step).start()
        return carry

    lax.fori_loop(1, per_group, send_out, 0)
    gathered[my_col] = mine[my_place]

    def wait_out(step, carry):
        col = lax.rem(my_col + step, col_blocks)
        pltpu.make_async_remote_copy(
            src_ref=gathered.at[col], dst_ref=gathered.at[col],
            send_sem=o_send.at[0], recv_sem=o_recv.at[col],
            device_id={"src": me}, device_id_type=MESH).wait_recv()
        return carry

    lax.fori_loop(1, col_blocks, wait_out, 0)
    for pair in range(col_blocks // 2):
        out_ref[0, :, pair * WINDOW:(pair + 1) * WINDOW] = gathered[2 * pair] + pltpu.roll(
            gathered[2 * pair + 1], BLOCK, 1)

    def drain(step, carry):
        col = lax.rem(my_col + step, col_blocks)

        @pl.when(jnp.logical_not(is_self(col)))
        def _():
            field_copy(col, own_group, first_slot, step).wait_send()

        @pl.when(second_ok)
        def _():
            field_copy(col, second, second_slot, col_blocks + step).wait_send()

        return carry

    lax.fori_loop(0, col_blocks, drain, 0)

    def drain_taps(step, carry):
        taps_copy(step).wait_send()
        return carry

    lax.fori_loop(1, n_src, drain_taps, 0)

    def drain_out(step, carry):
        out_copy(step).wait_send()
        return carry

    lax.fori_loop(1, per_group, drain_out, 0)


def per_device(near_field, x_taps, y_taps, source_weight):
    n_src = lax.axis_size("src")
    n_tile = lax.axis_size("tile")
    _, local_rows, _, comps, width = near_field.shape
    _, _, ranks, tap_count = x_taps.shape
    rim = (tap_count - 1) // 2
    col_blocks = width // BLOCK
    per_group = BLOCK // local_rows
    assert WINDOW == BLOCK + 2 * rim and x_taps.shape[0] == 1
    assert n_src == col_blocks * (n_src * local_rows // BLOCK) and per_group == col_blocks

    rows_last = near_field[0].transpose(2, 1, 0, 3).reshape(2 * comps * local_rows, width)
    padded = jnp.pad(rows_last, ((0, 0), (rim, rim)))
    windows = jnp.stack([padded[:, BLOCK * k:BLOCK * k + WINDOW] for k in range(col_blocks)])

    high = lax.reduce_precision(source_weight, 8, 7)
    rest = source_weight - high
    middle = lax.reduce_precision(rest, 8, 7)
    low = rest - middle
    weights = jnp.broadcast_to(
        jnp.stack([high, middle, low], axis=1).astype(jnp.bfloat16), (4 * ranks, 3))
    taps = jnp.concatenate(
        [x_taps.reshape(2 * ranks, tap_count), y_taps.reshape(2 * ranks, tap_count)], axis=0)
    taps = jnp.concatenate([jnp.pad(taps, ((0, 0), (0, WINDOW - 3 - tap_count))), weights], axis=1)

    slots = WINDOW // local_rows
    dma = pltpu.SemaphoreType.DMA
    bf16, f32 = jnp.bfloat16, jnp.float32
    vmem = pl.BlockSpec(memory_space=pltpu.VMEM)
    dims = (n_src, n_tile, local_rows, comps, ranks, tap_count)
    return pl.pallas_call(
        functools.partial(kernel, dims),
        out_shape=jax.ShapeDtypeStruct((1, local_rows, width), f32),
        in_specs=[vmem, vmem],
        out_specs=vmem,
        scratch_shapes=[
            pltpu.VMEM((slots, 2 * comps * local_rows, WINDOW), bf16),
            pltpu.VMEM((n_src, 4 * ranks, WINDOW), bf16),
            pltpu.VMEM((2 * comps, WINDOW, WINDOW), f32),
            pltpu.VMEM((2 * comps * WINDOW, 2 * WINDOW), bf16),
            pltpu.VMEM((ranks * BLOCK, 2 * WINDOW), bf16),
            pltpu.VMEM((2 * BLOCK, 2 * ranks * WINDOW), bf16),
            pltpu.VMEM((comps * BLOCK, 2 * ranks * WINDOW), bf16),
            pltpu.VMEM((WINDOW, WINDOW), f32),
            pltpu.VMEM((per_group, local_rows, WINDOW), f32),
            pltpu.VMEM((col_blocks, local_rows, WINDOW), f32),
            dma((2 * col_blocks,)),
            dma((slots,)),
            dma,
            dma((n_src,)),
            dma((n_src,)),
            dma,
            dma((per_group,)),
            dma((col_blocks,)),
        ],
        compiler_params=pltpu.CompilerParams(collective_id=0, has_side_effects=True),
    )(windows, taps)


def solution(mesh):
    placed = (
        P(("group", "tile"), "src", None, None, None),
        P("src", None, None, None),
        P("src", None, None, None),
        P("src"),
    )
    return jax.shard_map(
        per_device,
        mesh=mesh,
        in_specs=placed,
        out_specs=P(("group", "tile"), "src", None),
        check_vma=False,
    )
```

time: 143 us -> 35.7 us (0.25)
  waiting for transfers between devices: 64.1 us -> 0 us
  blocking collectives: 33.1 us -> 0 us
  Pallas kernels: 0 us -> 27.4 us
  matrix products: 10.1 us -> 0 us
  between operations: 14.2 us -> 4.48 us
  local copies, waits for them, and re-layouts: 11.8 us -> 2.8 us
  other arithmetic: 6.23 us -> 0.69 us
  starting transfers between devices: 3.26 us -> 0 us
    reduce_scatter x1 -> x0, waiting for transfers between devices: 64.1 us -> none  [per_device(): summed = lax.psum_scatter(own_image, 'src', scatter_dimension=0, tiled=True)]
    all_gather x1 -> x0, blocking collectives: 33.1 us -> none  [per_device(): whole_tile = lax.all_gather(near_field, 'src', axis=1, tiled=True)]
    pallas_call x0 -> x1, Pallas kernels: none -> 27.4 us  [per_device(): pl.pallas_call(functools.partial(kernel, dims), out_shape=jax.ShapeDtypeS...]
    dot_general x5 -> x0, matrix products: 10.1 us -> none  [the longest x1 3.22 us: one_block(): jnp.einsum('xoiprk,kxprcw->xoicw', row_mats, window, preferred_element_ty...]
    ppermute x2 -> x0, local copies, waits for them, and re-layouts: 4.26 us -> none  [the longest x1 2.16 us: padded_2(): lax.ppermute(tail, axis, [(i, (i + 1) % count) for i in range(ends)])]
    another operation x5 -> x1, other arithmetic: 3.48 us -> 0.08 us  [per_device(): jnp.stack([high, middle, low], axis=1).astype(jnp.bfloat16)]
    ppermute x2 -> x0, starting transfers between devices: 3.26 us -> none  [the longest x1 1.98 us: padded_2(): lax.ppermute(tail, axis, [(i, (i + 1) % count) for i in range(ends)])]
    slice x4 -> x0, local copies, waits for them, and re-layouts: 2.8 us -> none  [the longest x1 1.13 us: column_pass(): pieces[:, :, :, 1:]]
  transfers between devices with their start and end apart: 3 -> 0, of which waited for: 1 -> 0; matrix products, arithmetic and copies ran while one was open for 7% -> 0% of each run, Pallas kernels for 0% -> 0%
where the time goes in v1:
time: 35.7 us; the launch traced here: 35.4 us
  Pallas kernels  27.4 us (77%)
  between operations  4.48 us (13%)
  local copies, waits for them, and re-layouts  2.8 us (8%)
  other arithmetic  0.69 us (2%)
    pallas_call x1, Pallas kernels, per_device(): pl.pallas_call(functools.partial(kernel, dims), out_shape=jax.ShapeDtypeS...  27.4 us
    unnamed x14, local copies, waits for them, and re-layouts  1.91 us
    transpose x1, local copies, waits for them, and re-layouts, per_device(): near_field[0].transpose(2, 1, 0, 3).reshape(2 * comps * local_rows, width)  0.81 us

profile of v1, /device:TPU:0, one launch (start us, length us, event | category | flops | bytes accessed | tf_op | source)
XLA Modules:
  0.0 35.4 jit_solution(15306144513122847142)
XLA Ops:
  0.0 0.8 %copy.5 = bf16[3,2,8,512]{3,2,1,0:T(8,128)(2,1)S(1)} copy(bf16[3,2,8,512]{3,1,0,2:T(2,128)(2,1)} %bitcast.46) | data formatting | bytes 98304 | tf_op jit(solution)/shard_map/transpose | solution.py:264
  0.8 0.1 constant_dynamic-update-slice_fusion.7
  0.9 0.1 constant_dynamic-update-slice_fusion.6
  1.0 0.1 constant_dynamic-update-slice_fusion.5
  1.0 0.1 constant_dynamic-update-slice_fusion.4
  1.1 0.1 constant_dynamic-update-slice_fusion.3
  1.2 0.1 constant_dynamic-update-slice_fusion.2
  1.3 0.1 constant_dynamic-update-slice_fusion.1
  1.4 0.1 constant_dynamic-update-slice_fusion.field_ref
  1.5 0.0 copy-start
  4.5 0.0 copy-start.2
  5.3 0.0 copy-start.1
  5.9 0.1 pad_maximum_fusion.1
  6.0 0.0 copy-done.2
  6.0 0.0 copy-done.1
  6.0 0.6 %pad_maximum_fusion.taps_ref = bf16[32,128]{1,0:T(8,128)(2,1)} fusion(bf16[32,125]{1,0:T(8,128)(2,1)S(1)} %fusion.4, bf16[128]{0:T(256)(128)(2,1)S(1)} %pad_maximum_fusion.1), kind=kLoop, calls=%fused_computation.22 | loop fusion | flops 16384 | bytes 16448 | tf_op jit(solution)/shard_map/concatenate | solution.py:276
  6.6 0.0 copy-done
  6.6 27.4 %shard_map.46 = f32[1,8,512]{2,1,0:T(8,128)} custom-call(bf16[8,48,128]{2,1,0:T(8,128)(2,1)} %copy-done, bf16[32,128]{1,0:T(8,128)(2,1)} %pad_maximum_fusion.taps_ref), custom_call_target="tpu_custom_call" | custom-call | tf_op jit(solution)/shard_map/pallas_call | solution.py:283
  34.0 1.3 %copy.15 = f32[1,8,512]{2,1,0:T(8,128)} copy(f32[1,8,512]{2,1,0:T(8,128)} %shard_map.46) | data formatting | bytes 32768
  (1 shorter events, 0.0 us)
Async XLA Ops:
  1.5 5.2 %copy-start = (bf16[8,48,128]{2,1,0:T(8,128)(2,1)}, bf16[8,48,128]{2,1,0:T(8,128)(2,1)S(1)}, u32[]{:S(2)}) copy-start(bf16[8,48,128]{2,1,0:T(8,128)(2,1)S(1)} %constant_dynamic-update-slice_fusion.field_ref) | copy-start | bytes 294916
  4.5 1.5 %copy-start.2 = (bf16[1,2,8,65]{3,2,1,0:T(8,128)(2,1)S(1)}, bf16[1,2,8,65]{3,2,1,0:T(8,128)(2,1)}, u32[]{:S(2)}) copy-start(bf16[1,2,8,65]{3,2,1,0:T(8,128)(2,1)} %param.5) | copy-start | bytes 6244
  5.3 0.8 %copy-start.1 = (bf16[1,2,8,65]{3,2,1,0:T(8,128)(2,1)S(1)}, bf16[1,2,8,65]{3,2,1,0:T(8,128)(2,1)}, u32[]{:S(2)}) copy-start(bf16[1,2,8,65]{3,2,1,0:T(8,128)(2,1)} %param.6) | copy-start | bytes 6244

commit v2 on v1

--- a/solution.py
+++ b/solution.py
@@ -18,10 +18,21 @@
     return pltpu.roll(spread, 0, 1, stride=1, stride_axis=0)
 
 
-def kernel(dims, field_ref, taps_ref, out_ref, window, taps_all, field32, fields,
+def kernel(dims, field_hbm, x_hbm, y_hbm, weight_hbm, out_ref, raw, x_raw, y_raw, weight,
+           stage, field_ref, taps_ref, window, taps_all, field32, fields,
            col_mat, row_mat, passed, acc, mine, gathered,
-           f_send, f_recv, f_self, t_send, t_recv, t_self, o_send, o_recv):
+           in_sem, f_send, f_recv, t_send, t_recv, o_send, o_recv):
     n_src, n_tile, local_rows, comps, ranks, tap_count = dims
+    rim = (WINDOW - BLOCK) // 2
+    width = raw.shape[-1]
+    loads = [
+        pltpu.make_async_copy(x_hbm, x_raw, in_sem.at[0]),
+        pltpu.make_async_copy(y_hbm, y_raw, in_sem.at[1]),
+        pltpu.make_async_copy(weight_hbm, weight, in_sem.at[2]),
+        pltpu.make_async_copy(field_hbm, raw, in_sem.at[3]),
+    ]
+    for load in loads:
+        load.start()
     slots = WINDOW // local_rows
     per_group = BLOCK // local_rows
     halo = (WINDOW - BLOCK) // 2 // local_rows
@@ -42,7 +53,31 @@
         return carry
 
     lax.fori_loop(1, devices, greet, 0)
-    pl.semaphore_wait(barrier, devices - 1)
+
+    for load in loads[:3]:
+        load.wait()
+    whole = weight[...]
+    high = whole.astype(jnp.bfloat16).astype(jnp.float32)
+    middle = (whole - high).astype(jnp.bfloat16).astype(jnp.float32)
+    low = whole - high - middle
+    lane = lax.broadcasted_iota(jnp.int32, (4 * ranks, WINDOW), 1)
+    spare = jnp.where(lane == WINDOW - 1, high, jnp.where(lane == WINDOW - 2, middle, low))
+    taps32 = acc.at[:4 * ranks]
+    taps32[...] = spare
+    for part in range(2):
+        taps32[part * ranks:(part + 1) * ranks, :tap_count] = x_raw[part].astype(jnp.float32)
+        taps32[(2 + part) * ranks:(3 + part) * ranks, :tap_count] = y_raw[part].astype(
+            jnp.float32)
+    taps_ref[...] = taps32[...].astype(jnp.bfloat16)
+
+    loads[3].wait()
+    edge = jnp.zeros((stage.shape[0], WINDOW), jnp.float32)
+    stage[:, :WINDOW] = edge
+    stage[:, width:width + WINDOW] = edge
+    for pair in range(raw.shape[0]):
+        stage[2 * pair:2 * pair + 2, rim:rim + width] = raw[pair].astype(jnp.float32)
+    for col in range(field_ref.shape[0]):
+        field_ref[col] = stage[:, col * BLOCK:col * BLOCK + WINDOW].astype(jnp.bfloat16)
 
     own_group = flat // per_group
     place = lax.rem(flat, per_group)
@@ -62,8 +97,6 @@
 
     first_slot = place + halo
     second_slot = jnp.where(upper, place + halo - per_group, place + halo + per_group)
-    self_copy = pltpu.make_async_copy(field_ref.at[my_col], window.at[first_slot], f_self)
-    self_taps = pltpu.make_async_copy(taps_ref, taps_all.at[me], t_self)
 
     def is_self(col):
         return own_group * col_blocks + col == flat
@@ -74,8 +107,7 @@
             send_sem=t_send.at[step], recv_sem=t_recv.at[me],
             device_id={"src": lax.rem(me + step, n_src)}, device_id_type=MESH)
 
-    self_copy.start()
-    self_taps.start()
+    pl.semaphore_wait(barrier, devices - 1)
 
     def send_fields(step, carry):
         col = lax.rem(my_col + step, col_blocks)
@@ -90,19 +122,23 @@
 
         return carry
 
-    lax.fori_loop(0, col_blocks, send_fields, 0)
-
     def send_taps(step, carry):
         taps_copy(step).start()
         return carry
 
     lax.fori_loop(1, n_src, send_taps, 0)
+    lax.fori_loop(0, col_blocks, send_fields, 0)
 
     first_block = (tile * groups + my_row) * per_group - halo
-    self_copy.wait()
+    window[first_slot] = field_ref[my_col]
+    taps_all[me] = taps_ref[...]
     for slot in range(slots):
         block = first_block + slot
         ok = jnp.logical_and(block >= 0, block < devices)
+
+        @pl.when(jnp.logical_not(ok))
+        def _():
+            window[slot] = jnp.zeros(window.shape[1:], window.dtype)
 
         @pl.when(jnp.logical_and(ok, block != flat))
         def _():
@@ -111,22 +147,12 @@
                 send_sem=f_send.at[0], recv_sem=f_recv.at[slot],
                 device_id={"src": me}, device_id_type=MESH).wait_recv()
 
-        rows = pl.ds(slot * local_rows, local_rows)
-
-        @pl.when(ok)
-        def _():
-            got = window[slot].astype(jnp.float32)
-            for part in range(2 * comps):
-                field32[part, rows, :] = got[part * local_rows:(part + 1) * local_rows]
-
-        @pl.when(jnp.logical_not(ok))
-        def _():
-            for part in range(2 * comps):
-                field32[part, rows, :] = jnp.zeros((local_rows, WINDOW), jnp.float32)
-
+    rows = local_rows * 2 * comps
+    for slot in range(slots):
+        field32[slot * rows:(slot + 1) * rows, :] = window[slot].astype(jnp.float32)
     for comp in range(comps):
-        real = field32[2 * comp]
-        imag = field32[2 * comp + 1]
+        real = field32[pl.ds(2 * comp, WINDOW, stride=2 * comps), :]
+        imag = field32[pl.ds(2 * comp + 1, WINDOW, stride=2 * comps), :]
         top = pl.ds(comp * WINDOW, WINDOW)
         low = pl.ds((comps + comp) * WINDOW, WINDOW)
         fields[top, :WINDOW] = real.astype(jnp.bfloat16)
@@ -134,8 +160,6 @@
         fields[low, :WINDOW] = imag.astype(jnp.bfloat16)
         fields[low, WINDOW:] = real.astype(jnp.bfloat16)
 
-    self_taps.wait()
-
     def wait_taps(step, carry):
         source = lax.rem(me + step, n_src)
         pltpu.make_async_remote_copy(
@@ -147,7 +171,6 @@
     lax.fori_loop(1, n_src, wait_taps, 0)
 
     acc[...] = jnp.zeros_like(acc)
-    lane = lax.broadcasted_iota(jnp.int32, (4 * ranks, WINDOW), 1)
 
     def one_source(source, carry):
         raw = taps_all[source].astype(jnp.float32)
@@ -261,34 +284,29 @@
     assert WINDOW == BLOCK + 2 * rim and x_taps.shape[0] == 1
     assert n_src == col_blocks * (n_src * local_rows // BLOCK) and per_group == col_blocks
 
-    rows_last = near_field[0].transpose(2, 1, 0, 3).reshape(2 * comps * local_rows, width)
-    padded = jnp.pad(rows_last, ((0, 0), (rim, rim)))
-    windows = jnp.stack([padded[:, BLOCK * k:BLOCK * k + WINDOW] for k in range(col_blocks)])
-
-    high = lax.reduce_precision(source_weight, 8, 7)
-    rest = source_weight - high
-    middle = lax.reduce_precision(rest, 8, 7)
-    low = rest - middle
-    weights = jnp.broadcast_to(
-        jnp.stack([high, middle, low], axis=1).astype(jnp.bfloat16), (4 * ranks, 3))
-    taps = jnp.concatenate(
-        [x_taps.reshape(2 * ranks, tap_count), y_taps.reshape(2 * ranks, tap_count)], axis=0)
-    taps = jnp.concatenate([jnp.pad(taps, ((0, 0), (0, WINDOW - 3 - tap_count))), weights], axis=1)
-
+    rows_last = near_field[0].transpose(0, 2, 1, 3).reshape(comps * local_rows, 2, width)
     slots = WINDOW // local_rows
     dma = pltpu.SemaphoreType.DMA
     bf16, f32 = jnp.bfloat16, jnp.float32
     vmem = pl.BlockSpec(memory_space=pltpu.VMEM)
+    anywhere = pl.BlockSpec(memory_space=pl.ANY)
     dims = (n_src, n_tile, local_rows, comps, ranks, tap_count)
     return pl.pallas_call(
         functools.partial(kernel, dims),
         out_shape=jax.ShapeDtypeStruct((1, local_rows, width), f32),
-        in_specs=[vmem, vmem],
+        in_specs=[anywhere] * 4,
         out_specs=vmem,
         scratch_shapes=[
+            pltpu.VMEM((comps * local_rows, 2, width), bf16),
+            pltpu.VMEM((2, ranks, tap_count), bf16),
+            pltpu.VMEM((2, ranks, tap_count), bf16),
+            pltpu.VMEM((1, 1), f32),
+            pltpu.VMEM((2 * comps * local_rows, width + WINDOW), f32),
+            pltpu.VMEM((col_blocks, 2 * comps * local_rows, WINDOW), bf16),
+            pltpu.VMEM((4 * ranks, WINDOW), bf16),
             pltpu.VMEM((slots, 2 * comps * local_rows, WINDOW), bf16),
             pltpu.VMEM((n_src, 4 * ranks, WINDOW), bf16),
-            pltpu.VMEM((2 * comps, WINDOW, WINDOW), f32),
+            pltpu.VMEM((2 * comps * WINDOW, WINDOW), f32),
             pltpu.VMEM((2 * comps * WINDOW, 2 * WINDOW), bf16),
             pltpu.VMEM((ranks * BLOCK, 2 * WINDOW), bf16),
             pltpu.VMEM((2 * BLOCK, 2 * ranks * WINDOW), bf16),
@@ -296,17 +314,16 @@
             pltpu.VMEM((WINDOW, WINDOW), f32),
             pltpu.VMEM((per_group, local_rows, WINDOW), f32),
             pltpu.VMEM((col_blocks, local_rows, WINDOW), f32),
+            dma((4,)),
             dma((2 * col_blocks,)),
             dma((slots,)),
-            dma,
             dma((n_src,)),
             dma((n_src,)),
-            dma,
             dma((per_group,)),
             dma((col_blocks,)),
         ],
         compiler_params=pltpu.CompilerParams(collective_id=0, has_side_effects=True),
-    )(windows, taps)
+    )(rows_last, x_taps[0], y_taps[0], source_weight.reshape(1, 1))
 
 
 def solution(mesh):

time: 35.7 us -> 29 us (0.81)
  between operations: 4.48 us -> 0.66 us
  local copies, waits for them, and re-layouts: 2.8 us -> 1.32 us
  other arithmetic: 0.69 us -> 0 us
  Pallas kernels: 27.4 us -> 26.8 us
    transpose x1 -> x0, local copies, waits for them, and re-layouts: 0.81 us -> none  [per_device(): near_field[0].transpose(2, 1, 0, 3).reshape(2 * comps * local_rows, width)]
    pallas_call x1, Pallas kernels: 27.4 us -> 26.8 us  [per_device(): pl.pallas_call(functools.partial(kernel, dims), out_shape=jax.ShapeDtypeS...]
    concatenate x2 -> x0, other arithmetic: 0.61 us -> none  [the longest x1 0.61 us: per_device(): jnp.concatenate([jnp.pad(taps, ((0, 0), (0, WINDOW - 3 - tap_count))), we...]
    unnamed x14 -> x1, local copies, waits for them, and re-layouts: 1.91 us -> 1.32 us
where the time goes in v2:
time: 29 us; the launch traced here: 28.7 us
  Pallas kernels  26.8 us (92%)
  local copies, waits for them, and re-layouts  1.32 us (5%)
  between operations  0.66 us (2%)
    pallas_call x1, Pallas kernels, per_device(): pl.pallas_call(functools.partial(kernel, dims), out_shape=jax.ShapeDtypeS...  26.8 us
    unnamed x1, local copies, waits for them, and re-layouts  1.32 us

profile of v2, /device:TPU:0, one launch (start us, length us, event | category | flops | bytes accessed | tf_op | source)
XLA Modules:
  0.0 28.7 jit_solution(13498755648487201507)
XLA Ops:
  0.7 26.8 %shard_map.46 = f32[1,8,512]{2,1,0:T(8,128)} custom-call(bf16[24,2,512]{2,1,0:T(2,128)(2,1)} %bitcast.9, bf16[2,8,65]{2,1,0:T(8,128)(2,1)} %bitcast.10, bf16[2,8,65]{2,1,0:T(8,128)(2,1)} %bitcast.11, f32[1,1]{1,0:T(1,128)} %bitcast.8.weight_hbm), custom_call_target="tpu_custom_call" | custom-call | tf_op jit(solution)/shard_map/pallas_call | solution.py:294
  27.4 1.3 %copy.7 = f32[1,8,512]{2,1,0:T(8,128)} copy(f32[1,8,512]{2,1,0:T(8,128)} %shard_map.46) | data formatting | bytes 32768

commit v3 on v2

--- a/solution.py
+++ b/solution.py
@@ -11,6 +11,8 @@
 BLOCK = 64
 WINDOW = 128
 NT = (((1,), (1,)), ((), ()))
+HEAD = 1
+TURNS = 7
 
 
 def toeplitz(row):
@@ -122,12 +124,13 @@
 
         return carry
 
+    lax.fori_loop(0, col_blocks, send_fields, 0)
+
     def send_taps(step, carry):
         taps_copy(step).start()
         return carry
 
     lax.fori_loop(1, n_src, send_taps, 0)
-    lax.fori_loop(0, col_blocks, send_fields, 0)
 
     first_block = (tile * groups + my_row) * per_group - halo
     window[first_slot] = field_ref[my_col]
@@ -168,11 +171,10 @@
             device_id={"src": source}, device_id_type=MESH).wait_recv()
         return carry
 
-    lax.fori_loop(1, n_src, wait_taps, 0)
 
     acc[...] = jnp.zeros_like(acc)
 
-    def one_source(source, carry):
+    def one_source(source, slot):
         raw = taps_all[source].astype(jnp.float32)
         taps = jnp.where(lane < tap_count, raw, 0.0)
         weight = jnp.sum(
@@ -181,35 +183,51 @@
             across = pl.ds(rank * BLOCK, BLOCK)
             for part in range(2):
                 index = part * ranks + rank
-                col_mat[across, part * WINDOW:(part + 1) * WINDOW] = toeplitz(
+                col_mat[slot, across, part * WINDOW:(part + 1) * WINDOW] = toeplitz(
                     taps[index:index + 1]).astype(jnp.bfloat16)
             real = toeplitz(taps[2 * ranks + rank:2 * ranks + rank + 1])
             imag = toeplitz(taps[3 * ranks + rank:3 * ranks + rank + 1])
             base = 2 * rank * WINDOW
-            row_mat[:BLOCK, base:base + WINDOW] = real.astype(jnp.bfloat16)
-            row_mat[:BLOCK, base + WINDOW:base + 2 * WINDOW] = (-imag).astype(jnp.bfloat16)
-            row_mat[BLOCK:, base:base + WINDOW] = imag.astype(jnp.bfloat16)
-            row_mat[BLOCK:, base + WINDOW:base + 2 * WINDOW] = real.astype(jnp.bfloat16)
+            row_mat[slot, :BLOCK, base:base + WINDOW] = real.astype(jnp.bfloat16)
+            row_mat[slot, :BLOCK, base + WINDOW:base + 2 * WINDOW] = (-imag).astype(jnp.bfloat16)
+            row_mat[slot, BLOCK:, base:base + WINDOW] = imag.astype(jnp.bfloat16)
+            row_mat[slot, BLOCK:, base + WINDOW:base + 2 * WINDOW] = real.astype(jnp.bfloat16)
         for pair in range(comps):
             some = lax.dot_general(
-                col_mat[...], fields[2 * pair * WINDOW:2 * (pair + 1) * WINDOW, :], NT,
+                col_mat[slot], fields[2 * pair * WINDOW:2 * (pair + 1) * WINDOW, :], NT,
                 preferred_element_type=jnp.float32).astype(jnp.bfloat16)
             for half in range(2):
                 part, comp = divmod(2 * pair + half, comps)
                 for rank in range(ranks):
                     base = (2 * rank + part) * WINDOW
-                    passed[comp * BLOCK:(comp + 1) * BLOCK, base:base + WINDOW] = some[
+                    passed[slot, comp * BLOCK:(comp + 1) * BLOCK, base:base + WINDOW] = some[
                         rank * BLOCK:(rank + 1) * BLOCK, half * WINDOW:(half + 1) * WINDOW]
         image = lax.dot_general(
-            passed[...], row_mat[...], NT, preferred_element_type=jnp.float32)
+            passed[slot], row_mat[slot], NT, preferred_element_type=jnp.float32)
         power = image * image
         total = power[:BLOCK]
         for comp in range(1, comps):
             total = total + power[comp * BLOCK:(comp + 1) * BLOCK]
-        acc[:BLOCK, :] += weight * total
-        return carry
-
-    lax.fori_loop(0, n_src, one_source, 0)
+        return weight * total
+
+    def sources_from(first, count):
+        total = None
+        for turn in range(count):
+            term = one_source(lax.rem(me + first + turn, n_src), turn)
+            total = term if total is None else total + term
+        acc[:BLOCK, :] += total
+
+    def later_sources(step, carry):
+        sources_from(HEAD + step * TURNS, TURNS)
+        return carry
+
+    lax.fori_loop(1, HEAD, wait_taps, 0)
+    sources_from(0, HEAD)
+    lax.fori_loop(HEAD, n_src, wait_taps, 0)
+    rounds, rest = divmod(n_src - HEAD, TURNS)
+    lax.fori_loop(0, rounds, later_sources, 0)
+    if rest > 0:
+        sources_from(HEAD + rounds * TURNS, rest)
 
     turned = acc[...].T
     block_image = turned[:BLOCK] + turned[BLOCK:]
@@ -293,7 +311,7 @@
     dims = (n_src, n_tile, local_rows, comps, ranks, tap_count)
     return pl.pallas_call(
         functools.partial(kernel, dims),
-        out_shape=jax.ShapeDtypeStruct((1, local_rows, width), f32),
+        out_shape=pltpu.VMEM((1, local_rows, width), f32),
         in_specs=[anywhere] * 4,
         out_specs=vmem,
         scratch_shapes=[
@@ -308,9 +326,9 @@
             pltpu.VMEM((n_src, 4 * ranks, WINDOW), bf16),
             pltpu.VMEM((2 * comps * WINDOW, WINDOW), f32),
             pltpu.VMEM((2 * comps * WINDOW, 2 * WINDOW), bf16),
-            pltpu.VMEM((ranks * BLOCK, 2 * WINDOW), bf16),
-            pltpu.VMEM((2 * BLOCK, 2 * ranks * WINDOW), bf16),
-            pltpu.VMEM((comps * BLOCK, 2 * ranks * WINDOW), bf16),
+            pltpu.VMEM((TURNS, ranks * BLOCK, 2 * WINDOW), bf16),
+            pltpu.VMEM((TURNS, 2 * BLOCK, 2 * ranks * WINDOW), bf16),
+            pltpu.VMEM((TURNS, comps * BLOCK, 2 * ranks * WINDOW), bf16),
             pltpu.VMEM((WINDOW, WINDOW), f32),
             pltpu.VMEM((per_group, local_rows, WINDOW), f32),
             pltpu.VMEM((col_blocks, local_rows, WINDOW), f32),

time: 29 us -> 22.9 us (0.79)
  Pallas kernels: 26.8 us -> 21.4 us
  local copies, waits for them, and re-layouts: 1.32 us -> 0.61 us
    pallas_call x1, Pallas kernels: 26.8 us -> 21.4 us  [per_device(): pl.pallas_call(functools.partial(kernel, dims), out_shape=pltpu.VMEM((1,...]
    unnamed x1, local copies, waits for them, and re-layouts: 1.32 us -> 0.61 us
where the time goes in v3:
time: 22.9 us; the launch traced here: 22.7 us
  Pallas kernels  21.4 us (93%)
  between operations  0.66 us (3%)
  local copies, waits for them, and re-layouts  0.61 us (3%)
    pallas_call x1, Pallas kernels, per_device(): pl.pallas_call(functools.partial(kernel, dims), out_shape=pltpu.VMEM((1,...  21.4 us
    unnamed x1, local copies, waits for them, and re-layouts  0.61 us

profile of v3, /device:TPU:0, one launch (start us, length us, event | category | flops | bytes accessed | tf_op | source)
XLA Modules:
  0.0 22.7 jit_solution(10571666996799830105)
XLA Ops:
  0.7 21.4 %shard_map.46 = f32[1,8,512]{2,1,0:T(8,128)S(1)} custom-call(bf16[24,2,512]{2,1,0:T(2,128)(2,1)} %bitcast.9, bf16[2,8,65]{2,1,0:T(8,128)(2,1)} %bitcast.10, bf16[2,8,65]{2,1,0:T(8,128)(2,1)} %bitcast.11, f32[1,1]{1,0:T(1,128)} %bitcast.8.weight_hbm), custom_call_target="tpu_custom_call" | custom-call | tf_op jit(solution)/shard_map/pallas_call | solution.py:312
  22.1 0.6 %copy.6 = f32[1,8,512]{2,1,0:T(8,128)} copy(f32[1,8,512]{2,1,0:T(8,128)S(1)} %shard_map.46) | data formatting | bytes 32768

commit v4 on v3

--- a/solution.py
+++ b/solution.py
@@ -174,7 +174,7 @@
 
     acc[...] = jnp.zeros_like(acc)
 
-    def one_source(source, slot):
+    def column_pass(source, slot):
         raw = taps_all[source].astype(jnp.float32)
         taps = jnp.where(lane < tap_count, raw, 0.0)
         weight = jnp.sum(
@@ -202,6 +202,9 @@
                     base = (2 * rank + part) * WINDOW
                     passed[slot, comp * BLOCK:(comp + 1) * BLOCK, base:base + WINDOW] = some[
                         rank * BLOCK:(rank + 1) * BLOCK, half * WINDOW:(half + 1) * WINDOW]
+        return weight
+
+    def row_pass(weight, slot):
         image = lax.dot_general(
             passed[slot], row_mat[slot], NT, preferred_element_type=jnp.float32)
         power = image * image
@@ -211,10 +214,13 @@
         return weight * total
 
     def sources_from(first, count):
-        total = None
-        for turn in range(count):
-            term = one_source(lax.rem(me + first + turn, n_src), turn)
-            total = term if total is None else total + term
+        total = jnp.zeros((BLOCK, WINDOW), jnp.float32)
+        weights = []
+        for turn in range(count + 1):
+            if turn < count:
+                weights.append(column_pass(lax.rem(me + first + turn, n_src), turn))
+            if turn > 0:
+                total = total + row_pass(weights[turn - 1], turn - 1)
         acc[:BLOCK, :] += total
 
     def later_sources(step, carry):

time: 22.9 us -> 22.7 us (level)
  no operation moved by 1% of the time
where the time goes in v4:
time: 22.7 us; the launch traced here: 22.5 us
  Pallas kernels  21.2 us (93%)
  between operations  0.66 us (3%)
  local copies, waits for them, and re-layouts  0.61 us (3%)
    pallas_call x1, Pallas kernels, per_device(): pl.pallas_call(functools.partial(kernel, dims), out_shape=pltpu.VMEM((1,...  21.2 us
    unnamed x1, local copies, waits for them, and re-layouts  0.61 us

profile of v4, /device:TPU:0, one launch (start us, length us, event | category | flops | bytes accessed | tf_op | source)
XLA Modules:
  0.0 22.5 jit_solution(16376241106072710319)
XLA Ops:
  0.7 21.2 %shard_map.46 = f32[1,8,512]{2,1,0:T(8,128)S(1)} custom-call(bf16[24,2,512]{2,1,0:T(2,128)(2,1)} %bitcast.9, bf16[2,8,65]{2,1,0:T(8,128)(2,1)} %bitcast.10, bf16[2,8,65]{2,1,0:T(8,128)(2,1)} %bitcast.11, f32[1,1]{1,0:T(1,128)} %bitcast.8.weight_hbm), custom_call_target="tpu_custom_call" | custom-call | tf_op jit(solution)/shard_map/pallas_call | solution.py:318
  21.9 0.6 %copy.6 = f32[1,8,512]{2,1,0:T(8,128)} copy(f32[1,8,512]{2,1,0:T(8,128)S(1)} %shard_map.46) | data formatting | bytes 32768
